TPU v7x, 256 devices: a whole 4x4x8 slice. The times are simulated.
256 devices in a mesh: section: 8 (over x, core), blk: 32 (over y, z).
Axes of the slice: x: 4, y: 4, z: 8, core: 2. Of those that a mesh axis runs over, the one named last changes fastest.
Arguments:
- hidden: bfloat16 [16384, 1536], P('blk'), may hold values from -6 to 6
- stale_kv: bfloat16 [8, 16384, 3072], P('section', 'blk'), may hold values from -6 to 6
- w_qkv: bfloat16 [8, 1536, 4608], P('section', 'blk'), may hold values from -0.15625 to 0.15625
- w_out: bfloat16 [8, 1536, 1536], P('section', 'blk'), may hold values from -0.15625 to 0.15625
- q_gain: float32 [8, 128], P('section'), may hold values from 0.25 to 1.75
- k_gain: float32 [8, 128], P('section'), may hold values from 0.25 to 1.75
- mod_table: float32 [8, 16, 3, 1536], P('section'), may hold values from -4 to 4
- pattern: int32 [128, 8], P('blk'), may hold values from 0 to 1, as said below
- step_index: int32 [128], P('blk'), may hold values from 0 to 15
- order: int32 [4], replicated, may hold values from 0 to 3, each once
Outputs:
- layer_out: bfloat16 [8, 16384, 1536], P('section', 'blk')
- kv_cache: bfloat16 [8, 16384, 3072], P('section', 'blk')
Inputs may be any that keep to these rules, and one draw needn't show every extreme that they name: `pattern`: every row of the query tile's own tile (candidate c = tile index mod 4) is 1. `order`: names each patch once.
All inputs are finite; a program needn't handle non-finite values.
Results may differ from a plain program's by a relative error of at most 0.01.
Values may be sent and summed in bfloat16 or wider, within the bound.
A program may use at most 128 MiB of HBM per device.

v0:
```python
import math
import jax
import jax.numpy as jnp
from jax import lax
from jax.sharding import PartitionSpec as P

D = 1536
HEADS = 12
HDIM = 128
TILE = 128
PATCHES = 4
TSTEPS = 16
TOK_DEV = 128
NORM_EPS = 1e-06


def shifted(value, axis, steps):
    count = lax.axis_size(axis)
    pairs = [(source, (source + steps) % count) for source in range(count)]
    return lax.ppermute(value, axis, pairs)


def shifted_2(x, axis, by):
    count = lax.axis_size(axis)
    pairs = [(i, i + by) for i in range(count) if 0 <= i + by < count]
    return lax.ppermute(x, axis, pairs)


def layer_norm(values):
    centre = values - jnp.mean(values, axis=-1, keepdims=True)
    spread = jnp.mean(centre * centre, axis=-1, keepdims=True)
    return centre * lax.rsqrt(spread + NORM_EPS)


def head_norm(values, gain_row):
    square = jnp.mean(values * values, axis=-1, keepdims=True)
    return values * lax.rsqrt(square + NORM_EPS) * gain_row


def on_device(
    hidden, stale_kv, w_qkv, w_out, q_gain, k_gain, mod_table, pattern, step_index, order
):
    inner_width = HEADS * HDIM
    rows_patch = TOK_DEV
    tiles_patch = rows_patch // TILE
    candidate_tiles = pattern.shape[1]
    sections = lax.axis_size("section")
    section_id = lax.axis_index("section")
    full_qkv, full_out = (
        lax.all_gather(w_qkv[0], "blk", axis=0, tiled=True),
        lax.all_gather(w_out[0], "blk", axis=0, tiled=True),
    )
    query_gain = q_gain[0]
    key_gain = k_gain[0]
    modulation_table = mod_table[0].reshape(TSTEPS, 3 * D)
    tile_masks = pattern.reshape(PATCHES, tiles_patch, candidate_tiles)
    steps_tiles = step_index.reshape(PATCHES, tiles_patch)
    input_rows = hidden.reshape(PATCHES, rows_patch, D)
    own_store = stale_kv[0].reshape(PATCHES, rows_patch, 2 * inner_width)
    near_store = shifted(own_store, "blk", 1)
    received = jnp.zeros((rows_patch, D), jnp.bfloat16)
    results = jnp.zeros((PATCHES, rows_patch, D), jnp.bfloat16)
    inverse_root = 1.0 / math.sqrt(HDIM)

    def slot_step(slot, state_now):
        received, own_store, near_store, results = state_now
        offset = slot - section_id
        active = jnp.logical_and(offset >= 0, offset < PATCHES)
        clipped = jnp.clip(offset, 0, PATCHES - 1)
        patch_id = jnp.sum(jnp.where(jnp.arange(PATCHES) == clipped, order, 0))
        tokens = jnp.where(
            section_id == 0,
            lax.dynamic_index_in_dim(input_rows, patch_id, 0, keepdims=False),
            received,
        )
        tile_steps = lax.dynamic_index_in_dim(steps_tiles, patch_id, 0, keepdims=False)
        one_hot = (tile_steps[:, None] == jnp.arange(TSTEPS)[None, :]).astype(jnp.float32)
        modulation = jnp.dot(one_hot, modulation_table, precision=lax.Precision.HIGHEST)
        modulation = jnp.broadcast_to(modulation[:, None, :], (tiles_patch, TILE, 3 * D)).reshape(
            rows_patch, 3 * D
        )
        shift_term = modulation[:, :D]
        scale_term = modulation[:, D : 2 * D]
        gate_term = modulation[:, 2 * D :]

        def project(token_rows):
            modulated = (
                layer_norm(token_rows.astype(jnp.float32)) * (1.0 + scale_term) + shift_term
            ).astype(jnp.bfloat16)
            qkv = jnp.dot(modulated, full_qkv, preferred_element_type=jnp.float32)
            queries = head_norm(
                qkv[:, :inner_width].reshape(rows_patch, HEADS, HDIM), query_gain
            ).astype(jnp.bfloat16)
            return (modulated, queries, qkv[:, inner_width:].astype(jnp.bfloat16))

        def spare_project(token_rows):
            return (
                jnp.zeros((rows_patch, D), jnp.bfloat16),
                jnp.zeros((rows_patch, HEADS, HDIM), jnp.bfloat16),
                jnp.zeros((rows_patch, 2 * inner_width), jnp.bfloat16),
            )

        modulated, queries, fresh_kv = lax.cond(active, project, spare_project, tokens)
        own_store = jnp.where(
            active, lax.dynamic_update_index_in_dim(own_store, fresh_kv, patch_id, 0), own_store
        )
        near_fresh = shifted(fresh_kv, "blk", 1)
        near_store = jnp.where(
            active, lax.dynamic_update_index_in_dim(near_store, near_fresh, patch_id, 0), near_store
        )
        tile_mask = lax.dynamic_index_in_dim(tile_masks, patch_id, 0, keepdims=False)

        def attend(operands):
            token_rows, query_rows, own_rows, near_rows = operands
            candidates = jnp.concatenate(
                [own_rows.reshape(-1, 2 * inner_width), near_rows.reshape(-1, 2 * inner_width)],
                axis=0,
            )
            key_rows = head_norm(
                candidates[:, :inner_width].astype(jnp.float32).reshape(-1, HEADS, HDIM), key_gain
            ).astype(jnp.bfloat16)
            value_rows = candidates[:, inner_width:].reshape(-1, HEADS, HDIM)
            token_mask = jnp.broadcast_to(
                tile_mask.astype(jnp.float32)[:, None, :, None],
                (tiles_patch, TILE, candidate_tiles, TILE),
            ).reshape(rows_patch, candidate_tiles * TILE)
            scores = (
                jnp.einsum("qhd,khd->hqk", query_rows, key_rows, preferred_element_type=jnp.float32)
                * inverse_root
            )
            expo = jnp.exp(scores) * token_mask[None]
            weight_sum = jnp.sum(expo, axis=-1)
            mixture = jnp.einsum(
                "hqk,khd->qhd",
                expo.astype(jnp.bfloat16),
                value_rows,
                preferred_element_type=jnp.float32,
            )
            attended = (
                (mixture / jnp.transpose(weight_sum)[:, :, None])
                .reshape(rows_patch, inner_width)
                .astype(jnp.bfloat16)
            )
            projected = jnp.dot(attended, full_out, preferred_element_type=jnp.float32)
            return (token_rows.astype(jnp.float32) + gate_term * projected).astype(jnp.bfloat16)

        def spare_attend(operands):
            return jnp.zeros((rows_patch, D), jnp.bfloat16)

        output_rows = lax.cond(
            active, attend, spare_attend, (tokens, queries, own_store, near_store)
        )
        results = jnp.where(
            active, lax.dynamic_update_index_in_dim(results, output_rows, patch_id, 0), results
        )
        received = shifted_2(output_rows, "section", 1)
        return (received, own_store, near_store, results)

    slot_count = PATCHES + sections - 1
    received, own_store, near_store, results = lax.fori_loop(
        0, slot_count, slot_step, (received, own_store, near_store, results)
    )
    layer_out = results.reshape(1, PATCHES * rows_patch, D)
    kv_cache = own_store.reshape(1, PATCHES * rows_patch, 2 * inner_width)
    return (layer_out, kv_cache)


def solution(mesh):
    in_specs = (
        P("blk", None),
        P("section", "blk", None),
        P("section", "blk", None),
        P("section", "blk", None),
        P("section", None),
        P("section", None),
        P("section", None, None, None),
        P("blk", None),
        P("blk"),
        P(),
    )
    out_specs = (P("section", "blk", None), P("section", "blk", None))
    return jax.shard_map(
        on_device, mesh=mesh, in_specs=in_specs, out_specs=out_specs, check_vma=False
    )
```

profile of v0, /device:TPU:7, one launch (start us, length us, event | category | flops | bytes accessed | tf_op | source)
XLA Modules:
  0.0 1030.1 jit_solution(15740919164373035649)
XLA Ops:
  7.2 3.8 copy.63
  14.6 101.2 %collective-permute-done.2 = bf16[4,128,3072]{2,1,0:T(8,128)(2,1)} collective-permute-done((bf16[4,128,3072]{2,1,0:T(8,128)(2,1)}, bf16[4,128,3072]{2,1,0:T(8,128)(2,1)}, u32[]{:S(2)}, u32[]{:S(2)}) %collective-permute-start.2) | collective-permute-done | bytes 3145760 | tf_op jit(solution)/shard_map/ppermute | solution.py:20
  115.7 125.9 %all-gather.5.cloned.1.call-done = bf16[1,1536,4608]{2,1,0:T(8,128)(2,1)} async-done(((bf16[1,48,4608]{2,1,0:T(8,128)(2,1)}), bf16[1,1536,4608]{2,1,0:T(8,128)(2,1)}) %all-gather.5.cloned.1.call-update) | async-done | bytes 14155792 | tf_op jit(solution)/shard_map/all_gather | solution.py:50
  242.9 780.4 %while.20 = (s32[]{:T(128)}, bf16[128,1536]{1,0:T(8,128)(2,1)S(1)}, bf16[4,128,3072]{2,1,0:T(8,128)(2,1)}, bf16[4,128,3072]{2,1,0:T(8,128)(2,1)}, bf16[4,128,153...) while((s32[]{:T(128)}, bf16[128,1536]{1,0:T(8,128)(2,1)S(1)}, ...), condition=%wide.region_11.12_spmd, body=%wide.region_0.11_spmd.sunk | while | flops 3260855808 | bytes 107183792 | solution.py:160
  254.6 19.3 %collective-permute-done = bf16[128,3072]{1,0:T(8,128)(2,1)S(1)} collective-permute-done((bf16[128,3072]{1,0:T(8,128)(2,1)}, bf16[128,3072]{1,0:T(8,128)(2,1)S(1)}, u32[]{:S(2)}, u32[]{:S(2)}) %collective-permute-start) | collective-permute-done | bytes 786464 | tf_op jit(solution)/shard_map/while/body/eval_jaxpr/ppermute | solution.py:20
  294.6 14.4 %collective-permute-done = bf16[128,3072]{1,0:T(8,128)(2,1)S(1)} collective-permute-done((bf16[128,3072]{1,0:T(8,128)(2,1)}, bf16[128,3072]{1,0:T(8,128)(2,1)S(1)}, u32[]{:S(2)}, u32[]{:S(2)}) %collective-permute-start) | collective-permute-done | bytes 786464 | tf_op jit(solution)/shard_map/while/body/eval_jaxpr/ppermute | solution.py:20
  315.9 7.1 collective-permute-done.1
  334.6 13.3 %collective-permute-done = bf16[128,3072]{1,0:T(8,128)(2,1)S(1)} collective-permute-done((bf16[128,3072]{1,0:T(8,128)(2,1)}, bf16[128,3072]{1,0:T(8,128)(2,1)S(1)}, u32[]{:S(2)}, u32[]{:S(2)}) %collective-permute-start) | collective-permute-done | bytes 786464 | tf_op jit(solution)/shard_map/while/body/eval_jaxpr/ppermute | solution.py:20
  354.8 8.2 collective-permute-done.1
  374.6 14.4 %collective-permute-done = bf16[128,3072]{1,0:T(8,128)(2,1)S(1)} collective-permute-done((bf16[128,3072]{1,0:T(8,128)(2,1)}, bf16[128,3072]{1,0:T(8,128)(2,1)S(1)}, u32[]{:S(2)}, u32[]{:S(2)}) %collective-permute-start) | collective-permute-done | bytes 786464 | tf_op jit(solution)/shard_map/while/body/eval_jaxpr/ppermute | solution.py:20
  395.9 7.1 collective-permute-done.1
  414.6 14.4 %collective-permute-done = bf16[128,3072]{1,0:T(8,128)(2,1)S(1)} collective-permute-done((bf16[128,3072]{1,0:T(8,128)(2,1)}, bf16[128,3072]{1,0:T(8,128)(2,1)S(1)}, u32[]{:S(2)}, u32[]{:S(2)}) %collective-permute-start) | collective-permute-done | bytes 786464 | tf_op jit(solution)/shard_map/while/body/eval_jaxpr/ppermute | solution.py:20
  435.9 7.1 collective-permute-done.1
  454.6 14.4 %collective-permute-done = bf16[128,3072]{1,0:T(8,128)(2,1)S(1)} collective-permute-done((bf16[128,3072]{1,0:T(8,128)(2,1)}, bf16[128,3072]{1,0:T(8,128)(2,1)S(1)}, u32[]{:S(2)}, u32[]{:S(2)}) %collective-permute-start) | collective-permute-done | bytes 786464 | tf_op jit(solution)/shard_map/while/body/eval_jaxpr/ppermute | solution.py:20
  475.9 7.1 collective-permute-done.1
  494.6 12.2 %collective-permute-done = bf16[128,3072]{1,0:T(8,128)(2,1)S(1)} collective-permute-done((bf16[128,3072]{1,0:T(8,128)(2,1)}, bf16[128,3072]{1,0:T(8,128)(2,1)S(1)}, u32[]{:S(2)}, u32[]{:S(2)}) %collective-permute-start) | collective-permute-done | bytes 786464 | tf_op jit(solution)/shard_map/while/body/eval_jaxpr/ppermute | solution.py:20
  513.7 209.5 %collective-permute-done.1 = bf16[128,1536]{1,0:T(8,128)(2,1)S(1)} collective-permute-done((bf16[128,1536]{1,0:T(8,128)(2,1)}, bf16[128,1536]{1,0:T(8,128)(2,1)S(1)}, u32[]{:S(2)}, u32[]{:S(2)}) %collective-permute-start.1) | collective-permute-done | bytes 393248 | tf_op jit(solution)/shard_map/while/body/eval_jaxpr/ppermute | solution.py:26
  729.7 13.7 %conditional.4 = (bf16[128,12,128]{0,2,1:T(8,128)(2,1)}, bf16[128,3072]{1,0:T(8,128)(2,1)}, bf16[1,128,3072]{2,1,0:T(8,128)(2,1)}) conditional(s32[]{:T(128)} %convert_element_type.92, () %tuple.70, (bf16[128,1536]{1,0:T(8,128)(2,1)S(1)}, f32[4608]{0:T(1024)}, bf16[1536,4608]{1,0:T(8,128)(2,1)}, f32[1,128]{1,0:T(1,128)S(1)}) %tuple.71), branch_computations={%region_2.2_spmd, %region_3.6_spmd} | conditional | flops 1815284864 | bytes 26018840 | solution.py:103
  730.9 7.1 fusion.6
  745.9 11.9 %collective-permute-done = bf16[128,3072]{1,0:T(8,128)(2,1)S(1)} collective-permute-done((bf16[128,3072]{1,0:T(8,128)(2,1)}, bf16[128,3072]{1,0:T(8,128)(2,1)S(1)}, u32[]{:S(2)}, u32[]{:S(2)}) %collective-permute-start) | collective-permute-done | bytes 786464 | tf_op jit(solution)/shard_map/while/body/eval_jaxpr/ppermute | solution.py:20
  760.1 24.4 %conditional.5 = (bf16[128,1536]{1,0:T(8,128)(2,1)}, bf16[1,128,1536]{2,1,0:T(8,128)(2,1)}) conditional(s32[]{:T(128)} %convert_element_type.92, () %tuple.69, (bf16[128,1536]{1,0:T(8,128)(2,1)S(1)}, f32[4608]{0:T(1024)}, bf16[4,128,3072]{2,1,0:T(8,128)(2,1)}, bf16[4,128,3072]{2,1,0:T(8,128)(2,1)}, f32[1,128]{1,0:T(1,128)S(1)}, ...), branch_computations={%region_7.7_spmd, %region_8.10_spmd} | conditional | flops 1443506688 | bytes 69053088 | solution.py:150
  763.3 4.7 copy.31
  768.0 5.6 pad_maximum_fusion
  775.2 3.3 bitcast_reduce_fusion
  787.7 10.2 collective-permute-done.1
  804.5 13.7 %conditional.4 = (bf16[128,12,128]{0,2,1:T(8,128)(2,1)}, bf16[128,3072]{1,0:T(8,128)(2,1)}, bf16[1,128,3072]{2,1,0:T(8,128)(2,1)}) conditional(s32[]{:T(128)} %convert_element_type.92, () %tuple.70, (bf16[128,1536]{1,0:T(8,128)(2,1)S(1)}, f32[4608]{0:T(1024)}, bf16[1536,4608]{1,0:T(8,128)(2,1)}, f32[1,128]{1,0:T(1,128)S(1)}) %tuple.71), branch_computations={%region_2.2_spmd, %region_3.6_spmd} | conditional | flops 1815284864 | bytes 26018840 | solution.py:103
  805.7 7.1 fusion.6
  820.7 11.9 %collective-permute-done = bf16[128,3072]{1,0:T(8,128)(2,1)S(1)} collective-permute-done((bf16[128,3072]{1,0:T(8,128)(2,1)}, bf16[128,3072]{1,0:T(8,128)(2,1)S(1)}, u32[]{:S(2)}, u32[]{:S(2)}) %collective-permute-start) | collective-permute-done | bytes 786464 | tf_op jit(solution)/shard_map/while/body/eval_jaxpr/ppermute | solution.py:20
  834.8 24.4 %conditional.5 = (bf16[128,1536]{1,0:T(8,128)(2,1)}, bf16[1,128,1536]{2,1,0:T(8,128)(2,1)}) conditional(s32[]{:T(128)} %convert_element_type.92, () %tuple.69, (bf16[128,1536]{1,0:T(8,128)(2,1)S(1)}, f32[4608]{0:T(1024)}, bf16[4,128,3072]{2,1,0:T(8,128)(2,1)}, bf16[4,128,3072]{2,1,0:T(8,128)(2,1)}, f32[1,128]{1,0:T(1,128)S(1)}, ...), branch_computations={%region_7.7_spmd, %region_8.10_spmd} | conditional | flops 1443506688 | bytes 69053088 | solution.py:150
  838.0 4.7 copy.31
  842.8 5.6 pad_maximum_fusion
  849.9 3.3 bitcast_reduce_fusion
  862.5 12.3 %collective-permute-done.1 = bf16[128,1536]{1,0:T(8,128)(2,1)S(1)} collective-permute-done((bf16[128,1536]{1,0:T(8,128)(2,1)}, bf16[128,1536]{1,0:T(8,128)(2,1)S(1)}, u32[]{:S(2)}, u32[]{:S(2)}) %collective-permute-start.1) | collective-permute-done | bytes 393248 | tf_op jit(solution)/shard_map/while/body/eval_jaxpr/ppermute | solution.py:26
  881.4 13.7 %conditional.4 = (bf16[128,12,128]{0,2,1:T(8,128)(2,1)}, bf16[128,3072]{1,0:T(8,128)(2,1)}, bf16[1,128,3072]{2,1,0:T(8,128)(2,1)}) conditional(s32[]{:T(128)} %convert_element_type.92, () %tuple.70, (bf16[128,1536]{1,0:T(8,128)(2,1)S(1)}, f32[4608]{0:T(1024)}, bf16[1536,4608]{1,0:T(8,128)(2,1)}, f32[1,128]{1,0:T(1,128)S(1)}) %tuple.71), branch_computations={%region_2.2_spmd, %region_3.6_spmd} | conditional | flops 1815284864 | bytes 26018840 | solution.py:103
  882.6 7.2 fusion.6
  897.6 11.9 %collective-permute-done = bf16[128,3072]{1,0:T(8,128)(2,1)S(1)} collective-permute-done((bf16[128,3072]{1,0:T(8,128)(2,1)}, bf16[128,3072]{1,0:T(8,128)(2,1)S(1)}, u32[]{:S(2)}, u32[]{:S(2)}) %collective-permute-start) | collective-permute-done | bytes 786464 | tf_op jit(solution)/shard_map/while/body/eval_jaxpr/ppermute | solution.py:20
  911.7 24.4 %conditional.5 = (bf16[128,1536]{1,0:T(8,128)(2,1)}, bf16[1,128,1536]{2,1,0:T(8,128)(2,1)}) conditional(s32[]{:T(128)} %convert_element_type.92, () %tuple.69, (bf16[128,1536]{1,0:T(8,128)(2,1)S(1)}, f32[4608]{0:T(1024)}, bf16[4,128,3072]{2,1,0:T(8,128)(2,1)}, bf16[4,128,3072]{2,1,0:T(8,128)(2,1)}, f32[1,128]{1,0:T(1,128)S(1)}, ...), branch_computations={%region_7.7_spmd, %region_8.10_spmd} | conditional | flops 1443506688 | bytes 69053088 | solution.py:150
  914.9 4.7 copy.31
  919.7 5.6 pad_maximum_fusion
  926.8 3.3 bitcast_reduce_fusion
  939.4 14.8 %collective-permute-done.1 = bf16[128,1536]{1,0:T(8,128)(2,1)S(1)} collective-permute-done((bf16[128,1536]{1,0:T(8,128)(2,1)}, bf16[128,1536]{1,0:T(8,128)(2,1)S(1)}, u32[]{:S(2)}, u32[]{:S(2)}) %collective-permute-start.1) | collective-permute-done | bytes 393248 | tf_op jit(solution)/shard_map/while/body/eval_jaxpr/ppermute | solution.py:26
  960.8 13.7 %conditional.4 = (bf16[128,12,128]{0,2,1:T(8,128)(2,1)}, bf16[128,3072]{1,0:T(8,128)(2,1)}, bf16[1,128,3072]{2,1,0:T(8,128)(2,1)}) conditional(s32[]{:T(128)} %convert_element_type.92, () %tuple.70, (bf16[128,1536]{1,0:T(8,128)(2,1)S(1)}, f32[4608]{0:T(1024)}, bf16[1536,4608]{1,0:T(8,128)(2,1)}, f32[1,128]{1,0:T(1,128)S(1)}) %tuple.71), branch_computations={%region_2.2_spmd, %region_3.6_spmd} | conditional | flops 1815284864 | bytes 26018840 | solution.py:103
  962.0 7.1 fusion.6
  977.0 15.9 %collective-permute-done = bf16[128,3072]{1,0:T(8,128)(2,1)S(1)} collective-permute-done((bf16[128,3072]{1,0:T(8,128)(2,1)}, bf16[128,3072]{1,0:T(8,128)(2,1)S(1)}, u32[]{:S(2)}, u32[]{:S(2)}) %collective-permute-start) | collective-permute-done | bytes 786464 | tf_op jit(solution)/shard_map/while/body/eval_jaxpr/ppermute | solution.py:20
  995.1 24.4 %conditional.5 = (bf16[128,1536]{1,0:T(8,128)(2,1)}, bf16[1,128,1536]{2,1,0:T(8,128)(2,1)}) conditional(s32[]{:T(128)} %convert_element_type.92, () %tuple.69, (bf16[128,1536]{1,0:T(8,128)(2,1)S(1)}, f32[4608]{0:T(1024)}, bf16[4,128,3072]{2,1,0:T(8,128)(2,1)}, bf16[4,128,3072]{2,1,0:T(8,128)(2,1)}, f32[1,128]{1,0:T(1,128)S(1)}, ...), branch_computations={%region_7.7_spmd, %region_8.10_spmd} | conditional | flops 1443506688 | bytes 69053088 | solution.py:150
  998.3 4.7 copy.31
  1003.0 5.6 pad_maximum_fusion
  1010.1 3.3 bitcast_reduce_fusion
  (274 shorter events, 274.5 us)
Async XLA Ops:
  7.2 6.4 copy-start
  7.2 108.6 %all-gather.7.cloned.1.call-start = ((), (), s32[]{:S(2)}) async-start(), calls=%async_computation.1 | async-start | bytes 4866048 | tf_op jit(solution)/shard_map/all_gather | solution.py:51
  11.0 231.9 %copy-start.1 = (f32[1,128]{1,0:T(1,128)S(1)}, f32[1,128]{1,0:T(1,128)}, u32[]{:S(2)}) copy-start(f32[1,128]{1,0:T(1,128)} %param.20) | copy-start | bytes 1540
  11.0 231.9 %copy-start.2 = (s32[4]{0:T(128)S(1)}, s32[4]{0:T(128)}, u32[]{:S(2)}) copy-start(s32[4]{0:T(128)} %param.25) | copy-start | bytes 52
  11.0 231.9 %copy-start.3 = (s32[4]{0:T(128)S(1)}, s32[4]{0:T(128)}, u32[]{:S(2)}) copy-start(s32[4]{0:T(128)} %param.24) | copy-start | bytes 52
  11.0 231.9 %copy-start.4 = (f32[1,128]{1,0:T(1,128)S(1)}, f32[1,128]{1,0:T(1,128)}, u32[]{:S(2)}) copy-start(f32[1,128]{1,0:T(1,128)} %param.21) | copy-start | bytes 1540
  11.0 230.5 %all-gather.5.cloned.1.call-start = ((), (), s32[]{:S(2)}) async-start(), calls=%async_computation | async-start | bytes 14598144 | tf_op jit(solution)/shard_map/all_gather | solution.py:50
  11.8 103.9 %collective-permute-start.2 = (bf16[4,128,3072]{2,1,0:T(8,128)(2,1)}, bf16[4,128,3072]{2,1,0:T(8,128)(2,1)}, u32[]{:S(2)}, u32[]{:S(2)}) collective-permute-start(bf16[4,128,3072]{2,1,0:T(8,128)(2,1)} %bitcast.20), channel_id=1, source_target_pairs={{0,1},{1,2},{2,3},{3,4},{4,5},{5,6},{6,7},{7,8},{8,9},{9,10},{10,1... | collective-permute-start | bytes 9437192 | tf_op jit(solution)/shard_map/ppermute | solution.py:20
  252.4 21.5 %collective-permute-start = (bf16[128,3072]{1,0:T(8,128)(2,1)}, bf16[128,3072]{1,0:T(8,128)(2,1)S(1)}, u32[]{:S(2)}, u32[]{:S(2)}) collective-permute-start(bf16[128,3072]{1,0:T(8,128)(2,1)} %get-tuple-element.585), channel_id=1, source_target_pairs={{0,1},{1,2},{2,3},{3,4},{4,5},{5,6},{6,7},{7,8},{8,9},{9,10},{10,1... | collective-permute-start | bytes 2359304 | tf_op jit(solution)/shard_map/while/body/eval_jaxpr/ppermute | solution.py:20
  277.7 5.3 collective-permute-start.1
  292.4 16.6 %collective-permute-start = (bf16[128,3072]{1,0:T(8,128)(2,1)}, bf16[128,3072]{1,0:T(8,128)(2,1)S(1)}, u32[]{:S(2)}, u32[]{:S(2)}) collective-permute-start(bf16[128,3072]{1,0:T(8,128)(2,1)} %get-tuple-element.585), channel_id=1, source_target_pairs={{0,1},{1,2},{2,3},{3,4},{4,5},{5,6},{6,7},{7,8},{8,9},{9,10},{10,1... | collective-permute-start | bytes 2359304 | tf_op jit(solution)/shard_map/while/body/eval_jaxpr/ppermute | solution.py:20
  312.7 10.2 collective-permute-start.1
  332.4 15.5 %collective-permute-start = (bf16[128,3072]{1,0:T(8,128)(2,1)}, bf16[128,3072]{1,0:T(8,128)(2,1)S(1)}, u32[]{:S(2)}, u32[]{:S(2)}) collective-permute-start(bf16[128,3072]{1,0:T(8,128)(2,1)} %get-tuple-element.585), channel_id=1, source_target_pairs={{0,1},{1,2},{2,3},{3,4},{4,5},{5,6},{6,7},{7,8},{8,9},{9,10},{10,1... | collective-permute-start | bytes 2359304 | tf_op jit(solution)/shard_map/while/body/eval_jaxpr/ppermute | solution.py:20
  351.6 11.3 %collective-permute-start.1 = (bf16[128,1536]{1,0:T(8,128)(2,1)}, bf16[128,1536]{1,0:T(8,128)(2,1)S(1)}, u32[]{:S(2)}, u32[]{:S(2)}) collective-permute-start(bf16[128,1536]{1,0:T(8,128)(2,1)} %get-tuple-element.587), channel_id=1, source_target_pairs={{0,32},{32,64},{64,96},{96,128},{128,160},{160,192},{192,224},{1,3... | collective-permute-start | bytes 1179656 | tf_op jit(solution)/shard_map/while/body/eval_jaxpr/ppermute | solution.py:26
  372.4 16.6 %collective-permute-start = (bf16[128,3072]{1,0:T(8,128)(2,1)}, bf16[128,3072]{1,0:T(8,128)(2,1)S(1)}, u32[]{:S(2)}, u32[]{:S(2)}) collective-permute-start(bf16[128,3072]{1,0:T(8,128)(2,1)} %get-tuple-element.585), channel_id=1, source_target_pairs={{0,1},{1,2},{2,3},{3,4},{4,5},{5,6},{6,7},{7,8},{8,9},{9,10},{10,1... | collective-permute-start | bytes 2359304 | tf_op jit(solution)/shard_map/while/body/eval_jaxpr/ppermute | solution.py:20
  392.7 10.2 collective-permute-start.1
  412.4 16.6 %collective-permute-start = (bf16[128,3072]{1,0:T(8,128)(2,1)}, bf16[128,3072]{1,0:T(8,128)(2,1)S(1)}, u32[]{:S(2)}, u32[]{:S(2)}) collective-permute-start(bf16[128,3072]{1,0:T(8,128)(2,1)} %get-tuple-element.585), channel_id=1, source_target_pairs={{0,1},{1,2},{2,3},{3,4},{4,5},{5,6},{6,7},{7,8},{8,9},{9,10},{10,1... | collective-permute-start | bytes 2359304 | tf_op jit(solution)/shard_map/while/body/eval_jaxpr/ppermute | solution.py:20
  432.7 10.2 collective-permute-start.1
  452.4 16.6 %collective-permute-start = (bf16[128,3072]{1,0:T(8,128)(2,1)}, bf16[128,3072]{1,0:T(8,128)(2,1)S(1)}, u32[]{:S(2)}, u32[]{:S(2)}) collective-permute-start(bf16[128,3072]{1,0:T(8,128)(2,1)} %get-tuple-element.585), channel_id=1, source_target_pairs={{0,1},{1,2},{2,3},{3,4},{4,5},{5,6},{6,7},{7,8},{8,9},{9,10},{10,1... | collective-permute-start | bytes 2359304 | tf_op jit(solution)/shard_map/while/body/eval_jaxpr/ppermute | solution.py:20
  472.7 10.2 collective-permute-start.1
  492.4 14.4 %collective-permute-start = (bf16[128,3072]{1,0:T(8,128)(2,1)}, bf16[128,3072]{1,0:T(8,128)(2,1)S(1)}, u32[]{:S(2)}, u32[]{:S(2)}) collective-permute-start(bf16[128,3072]{1,0:T(8,128)(2,1)} %get-tuple-element.585), channel_id=1, source_target_pairs={{0,1},{1,2},{2,3},{3,4},{4,5},{5,6},{6,7},{7,8},{8,9},{9,10},{10,1... | collective-permute-start | bytes 2359304 | tf_op jit(solution)/shard_map/while/body/eval_jaxpr/ppermute | solution.py:20
  510.5 212.6 %collective-permute-start.1 = (bf16[128,1536]{1,0:T(8,128)(2,1)}, bf16[128,1536]{1,0:T(8,128)(2,1)S(1)}, u32[]{:S(2)}, u32[]{:S(2)}) collective-permute-start(bf16[128,1536]{1,0:T(8,128)(2,1)} %get-tuple-element.587), channel_id=1, source_target_pairs={{0,32},{32,64},{64,96},{96,128},{128,160},{160,192},{192,224},{1,3... | collective-permute-start | bytes 1179656 | tf_op jit(solution)/shard_map/while/body/eval_jaxpr/ppermute | solution.py:26
  743.5 14.4 %collective-permute-start = (bf16[128,3072]{1,0:T(8,128)(2,1)}, bf16[128,3072]{1,0:T(8,128)(2,1)S(1)}, u32[]{:S(2)}, u32[]{:S(2)}) collective-permute-start(bf16[128,3072]{1,0:T(8,128)(2,1)} %get-tuple-element.585), channel_id=1, source_target_pairs={{0,1},{1,2},{2,3},{3,4},{4,5},{5,6},{6,7},{7,8},{8,9},{9,10},{10,1... | collective-permute-start | bytes 2359304 | tf_op jit(solution)/shard_map/while/body/eval_jaxpr/ppermute | solution.py:20
  775.1 6.0 slice-start
  778.5 2.7 slice-start.1
  784.5 13.5 %collective-permute-start.1 = (bf16[128,1536]{1,0:T(8,128)(2,1)}, bf16[128,1536]{1,0:T(8,128)(2,1)S(1)}, u32[]{:S(2)}, u32[]{:S(2)}) collective-permute-start(bf16[128,1536]{1,0:T(8,128)(2,1)} %get-tuple-element.587), channel_id=1, source_target_pairs={{0,32},{32,64},{64,96},{96,128},{128,160},{160,192},{192,224},{1,3... | collective-permute-start | bytes 1179656 | tf_op jit(solution)/shard_map/while/body/eval_jaxpr/ppermute | solution.py:26
  818.3 14.4 %collective-permute-start = (bf16[128,3072]{1,0:T(8,128)(2,1)}, bf16[128,3072]{1,0:T(8,128)(2,1)S(1)}, u32[]{:S(2)}, u32[]{:S(2)}) collective-permute-start(bf16[128,3072]{1,0:T(8,128)(2,1)} %get-tuple-element.585), channel_id=1, source_target_pairs={{0,1},{1,2},{2,3},{3,4},{4,5},{5,6},{6,7},{7,8},{8,9},{9,10},{10,1... | collective-permute-start | bytes 2359304 | tf_op jit(solution)/shard_map/while/body/eval_jaxpr/ppermute | solution.py:20
  849.9 6.0 slice-start
  853.2 2.7 slice-start.1
  859.3 15.6 %collective-permute-start.1 = (bf16[128,1536]{1,0:T(8,128)(2,1)}, bf16[128,1536]{1,0:T(8,128)(2,1)S(1)}, u32[]{:S(2)}, u32[]{:S(2)}) collective-permute-start(bf16[128,1536]{1,0:T(8,128)(2,1)} %get-tuple-element.587), channel_id=1, source_target_pairs={{0,32},{32,64},{64,96},{96,128},{128,160},{160,192},{192,224},{1,3... | collective-permute-start | bytes 1179656 | tf_op jit(solution)/shard_map/while/body/eval_jaxpr/ppermute | solution.py:26
  895.2 14.4 %collective-permute-start = (bf16[128,3072]{1,0:T(8,128)(2,1)}, bf16[128,3072]{1,0:T(8,128)(2,1)S(1)}, u32[]{:S(2)}, u32[]{:S(2)}) collective-permute-start(bf16[128,3072]{1,0:T(8,128)(2,1)} %get-tuple-element.585), channel_id=1, source_target_pairs={{0,1},{1,2},{2,3},{3,4},{4,5},{5,6},{6,7},{7,8},{8,9},{9,10},{10,1... | collective-permute-start | bytes 2359304 | tf_op jit(solution)/shard_map/while/body/eval_jaxpr/ppermute | solution.py:20
  926.8 6.0 slice-start
  930.1 2.7 slice-start.1
  936.2 18.1 %collective-permute-start.1 = (bf16[128,1536]{1,0:T(8,128)(2,1)}, bf16[128,1536]{1,0:T(8,128)(2,1)S(1)}, u32[]{:S(2)}, u32[]{:S(2)}) collective-permute-start(bf16[128,1536]{1,0:T(8,128)(2,1)} %get-tuple-element.587), channel_id=1, source_target_pairs={{0,32},{32,64},{64,96},{96,128},{128,160},{160,192},{192,224},{1,3... | collective-permute-start | bytes 1179656 | tf_op jit(solution)/shard_map/while/body/eval_jaxpr/ppermute | solution.py:26
  974.5 18.3 %collective-permute-start = (bf16[128,3072]{1,0:T(8,128)(2,1)}, bf16[128,3072]{1,0:T(8,128)(2,1)S(1)}, u32[]{:S(2)}, u32[]{:S(2)}) collective-permute-start(bf16[128,3072]{1,0:T(8,128)(2,1)} %get-tuple-element.585), channel_id=1, source_target_pairs={{0,1},{1,2},{2,3},{3,4},{4,5},{5,6},{6,7},{7,8},{8,9},{9,10},{10,1... | collective-permute-start | bytes 2359304 | tf_op jit(solution)/shard_map/while/body/eval_jaxpr/ppermute | solution.py:20
  1010.1 6.0 slice-start
  1013.5 2.7 slice-start.1
  1019.5 3.8 collective-permute-start.1
Sparse Core Ops, SparseCore 0:
  11.2 102.6 all-gather.6
  116.4 125.1 all-gather.4
where the time goes:
time: 1030 us
  waiting for transfers between devices  668 us (65%)
  other arithmetic  126 us (12%)
  local copies, waits for them, and re-layouts  103 us (10%)
  matrix products  82.5 us (8%)
  loops' own time  20.9 us (2%)
  starting transfers between devices  15.9 us (2%)
  between operations  14.1 us (1%)
    ppermute x11, waiting for transfers between devices, shifted_2(): return lax.ppermute(x, axis, pairs)  286 us
    ppermute x12, waiting for transfers between devices, shifted(): return lax.ppermute(value, axis, pairs)  255 us
    all_gather x1, waiting for transfers between devices, on_device(): lax.all_gather(w_qkv[0], 'blk', axis=0, tiled=True)  126 us
    dot_general x4, matrix products, project(): qkv = jnp.dot(modulated, full_qkv, preferred_element_type=jnp.float32)  28.6 us
    dot_general x11, matrix products, slot_step(): jnp.dot(one_hot, modulation_table, precision=lax.Precision.HIGHEST)  26.6 us
    select_n x11, other arithmetic, slot_step(): jnp.where(active, lax.dynamic_update_index_in_dim(own_store, fresh_kv, pa...  25.1 us
    select_n x11, other arithmetic, slot_step(): jnp.where(active, lax.dynamic_update_index_in_dim(near_store, near_fresh,...  24.3 us
    concatenate x4, other arithmetic, attend(): jnp.concatenate([own_rows.reshape(-1, 2 * inner_width), near_rows.reshape...  22.5 us
  transfers between devices with their start and end apart: 25, of which 24 were waited for; matrix products, arithmetic and copies ran while one was open for 5% of the time, Pallas kernels for 0%

commit v1 on v0

--- a/solution.py
+++ b/solution.py
@@ -3,6 +3,7 @@
 import jax.numpy as jnp
 from jax import lax
 from jax.sharding import PartitionSpec as P
+from jax.lax import all_to_all, psum
 
 D = 1536
 HEADS = 12
@@ -12,6 +13,13 @@
 TSTEPS = 16
 TOK_DEV = 128
 NORM_EPS = 1e-06
+
+
+def target_derive(shard_in, which_axis):
+    t_next = jnp.stack([shard_in for _ in range(psum(1, which_axis))])
+    return jnp.concatenate(
+        all_to_all(t_next, axis_name=which_axis, split_axis=0, concat_axis=0), axis=0
+    )
 
 
 def shifted(value, axis, steps):
@@ -47,7 +55,7 @@
     sections = lax.axis_size("section")
     section_id = lax.axis_index("section")
     full_qkv, full_out = (
-        lax.all_gather(w_qkv[0], "blk", axis=0, tiled=True),
+        target_derive(w_qkv[0], "blk"),
         lax.all_gather(w_out[0], "blk", axis=0, tiled=True),
     )
     query_gain = q_gain[0]

time: 1030 us -> 1240 us (1.20)
  waiting for transfers between devices: 668 us -> 843 us
  starting transfers between devices: 15.9 us -> 33.6 us
    ppermute x12, waiting for transfers between devices: 255 us -> 553 us  [shifted(): return lax.ppermute(value, axis, pairs)]
    all_gather x1 -> x0, waiting for transfers between devices: 126 us -> none  [on_device(): lax.all_gather(w_qkv[0], 'blk', axis=0, tiled=True)]
  transfers between devices with their start and end apart: 25 -> 25, of which waited for: 24 -> 23; matrix products, arithmetic and copies ran while one was open for 5% -> 4% of each run, Pallas kernels for 0% -> 0%
where the time goes in v1:
time: 1240 us; the launch traced here: 1230 us
  waiting for transfers between devices  843 us (68%)
  other arithmetic  126 us (10%)
  local copies, waits for them, and re-layouts  110 us (9%)
  matrix products  82.8 us (7%)
  starting transfers between devices  33.6 us (3%)
  loops' own time  23.8 us (2%)
  between operations  14.1 us (1%)
    ppermute x12, waiting for transfers between devices, shifted(): return lax.ppermute(value, axis, pairs)  553 us
    ppermute x11, waiting for transfers between devices, shifted_2(): return lax.ppermute(x, axis, pairs)  289 us
    dot_general x4, matrix products, project(): qkv = jnp.dot(modulated, full_qkv, preferred_element_type=jnp.float32)  28.6 us
    dot_general x11, matrix products, slot_step(): jnp.dot(one_hot, modulation_table, precision=lax.Precision.HIGHEST)  26.8 us
    select_n x11, other arithmetic, slot_step(): jnp.where(active, lax.dynamic_update_index_in_dim(own_store, fresh_kv, pa...  25.1 us
  transfers between devices with their start and end apart: 25, of which 23 were waited for; matrix products, arithmetic and copies ran while one was open for 4% of the time, Pallas kernels for 0%

profile of v1, /device:TPU:7, one launch (start us, length us, event | category | flops | bytes accessed | tf_op | source)
XLA Modules:
  0.0 1233.1 jit_solution(15838335971762245686)
XLA Ops:
  7.2 3.8 copy.63
  11.0 6.7 stack.3
  17.7 11.5 all-to-all-start
  32.2 406.2 %collective-permute-done.2 = bf16[4,128,3072]{2,1,0:T(8,128)(2,1)} collective-permute-done((bf16[4,128,3072]{2,1,0:T(8,128)(2,1)}, bf16[4,128,3072]{2,1,0:T(8,128)(2,1)}, u32[]{:S(2)}, u32[]{:S(2)}) %collective-permute-start.2) | collective-permute-done | bytes 3145760 | tf_op jit(solution)/shard_map/ppermute | solution.py:28
  439.7 786.5 %while.20 = (s32[]{:T(128)}, bf16[128,1536]{1,0:T(8,128)(2,1)S(1)}, bf16[4,128,3072]{2,1,0:T(8,128)(2,1)}, bf16[4,128,3072]{2,1,0:T(8,128)(2,1)}, bf16[4,128,153...) while((s32[]{:T(128)}, bf16[128,1536]{1,0:T(8,128)(2,1)S(1)}, ...), condition=%wide.region_11.12_spmd, body=%wide.region_0.11_spmd.sunk | while | flops 3260855808 | bytes 107183792 | solution.py:168
  451.9 18.9 %collective-permute-done = bf16[128,3072]{1,0:T(8,128)(2,1)S(1)} collective-permute-done((bf16[128,3072]{1,0:T(8,128)(2,1)}, bf16[128,3072]{1,0:T(8,128)(2,1)S(1)}, u32[]{:S(2)}, u32[]{:S(2)}) %collective-permute-start) | collective-permute-done | bytes 786464 | tf_op jit(solution)/shard_map/while/body/eval_jaxpr/ppermute | solution.py:28
  490.0 6.8 collective-permute-start
  499.0 7.1 collective-permute-done
  513.0 14.5 %collective-permute-done.1 = bf16[128,1536]{1,0:T(8,128)(2,1)S(1)} collective-permute-done((bf16[128,1536]{1,0:T(8,128)(2,1)}, bf16[128,1536]{1,0:T(8,128)(2,1)S(1)}, u32[]{:S(2)}, u32[]{:S(2)}) %collective-permute-start.1) | collective-permute-done | bytes 393248 | tf_op jit(solution)/shard_map/while/body/eval_jaxpr/ppermute | solution.py:34
  539.4 14.2 %collective-permute-done = bf16[128,3072]{1,0:T(8,128)(2,1)S(1)} collective-permute-done((bf16[128,3072]{1,0:T(8,128)(2,1)}, bf16[128,3072]{1,0:T(8,128)(2,1)S(1)}, u32[]{:S(2)}, u32[]{:S(2)}) %collective-permute-start) | collective-permute-done | bytes 786464 | tf_op jit(solution)/shard_map/while/body/eval_jaxpr/ppermute | solution.py:28
  560.4 7.3 collective-permute-done.1
  579.7 14.4 %collective-permute-done = bf16[128,3072]{1,0:T(8,128)(2,1)S(1)} collective-permute-done((bf16[128,3072]{1,0:T(8,128)(2,1)}, bf16[128,3072]{1,0:T(8,128)(2,1)S(1)}, u32[]{:S(2)}, u32[]{:S(2)}) %collective-permute-start) | collective-permute-done | bytes 786464 | tf_op jit(solution)/shard_map/while/body/eval_jaxpr/ppermute | solution.py:28
  601.0 7.1 collective-permute-done.1
  620.0 14.4 %collective-permute-done = bf16[128,3072]{1,0:T(8,128)(2,1)S(1)} collective-permute-done((bf16[128,3072]{1,0:T(8,128)(2,1)}, bf16[128,3072]{1,0:T(8,128)(2,1)S(1)}, u32[]{:S(2)}, u32[]{:S(2)}) %collective-permute-start) | collective-permute-done | bytes 786464 | tf_op jit(solution)/shard_map/while/body/eval_jaxpr/ppermute | solution.py:28
  641.3 7.1 collective-permute-done.1
  660.3 14.4 %collective-permute-done = bf16[128,3072]{1,0:T(8,128)(2,1)S(1)} collective-permute-done((bf16[128,3072]{1,0:T(8,128)(2,1)}, bf16[128,3072]{1,0:T(8,128)(2,1)S(1)}, u32[]{:S(2)}, u32[]{:S(2)}) %collective-permute-start) | collective-permute-done | bytes 786464 | tf_op jit(solution)/shard_map/while/body/eval_jaxpr/ppermute | solution.py:28
  681.6 7.1 collective-permute-done.1
  700.7 12.2 collective-permute-done
  719.8 205.2 %collective-permute-done.1 = bf16[128,1536]{1,0:T(8,128)(2,1)S(1)} collective-permute-done((bf16[128,1536]{1,0:T(8,128)(2,1)}, bf16[128,1536]{1,0:T(8,128)(2,1)S(1)}, u32[]{:S(2)}, u32[]{:S(2)}) %collective-permute-start.1) | collective-permute-done | bytes 393248 | tf_op jit(solution)/shard_map/while/body/eval_jaxpr/ppermute | solution.py:34
  931.8 13.7 %conditional.4 = (bf16[128,12,128]{0,2,1:T(8,128)(2,1)}, bf16[128,3072]{1,0:T(8,128)(2,1)}, bf16[1,128,3072]{2,1,0:T(8,128)(2,1)}) conditional(s32[]{:T(128)} %convert_element_type.92, () %tuple.70, (bf16[128,1536]{1,0:T(8,128)(2,1)S(1)}, f32[4608]{0:T(1024)}, bf16[1536,4608]{1,0:T(8,128)(2,1)}, f32[1,128]{1,0:T(1,128)S(1)}) %tuple.71), branch_computations={%region_2.2_spmd, %region_3.6_spmd} | conditional | flops 1815284864 | bytes 26018840 | solution.py:111
  933.0 7.2 fusion.6
  948.0 11.9 collective-permute-done
  962.1 24.4 %conditional.5 = (bf16[128,1536]{1,0:T(8,128)(2,1)}, bf16[1,128,1536]{2,1,0:T(8,128)(2,1)}) conditional(s32[]{:T(128)} %convert_element_type.92, () %tuple.69, (bf16[128,1536]{1,0:T(8,128)(2,1)S(1)}, f32[4608]{0:T(1024)}, bf16[4,128,3072]{2,1,0:T(8,128)(2,1)}, bf16[4,128,3072]{2,1,0:T(8,128)(2,1)}, f32[1,128]{1,0:T(1,128)S(1)}, ...), branch_computations={%region_7.7_spmd, %region_8.10_spmd} | conditional | flops 1443506688 | bytes 69053088 | solution.py:158
  965.3 4.7 copy.31
  970.0 5.6 pad_maximum_fusion
  977.2 3.3 bitcast_reduce_fusion
  989.8 10.3 collective-permute-done.1
  1007.0 13.7 %conditional.4 = (bf16[128,12,128]{0,2,1:T(8,128)(2,1)}, bf16[128,3072]{1,0:T(8,128)(2,1)}, bf16[1,128,3072]{2,1,0:T(8,128)(2,1)}) conditional(s32[]{:T(128)} %convert_element_type.92, () %tuple.70, (bf16[128,1536]{1,0:T(8,128)(2,1)S(1)}, f32[4608]{0:T(1024)}, bf16[1536,4608]{1,0:T(8,128)(2,1)}, f32[1,128]{1,0:T(1,128)S(1)}) %tuple.71), branch_computations={%region_2.2_spmd, %region_3.6_spmd} | conditional | flops 1815284864 | bytes 26018840 | solution.py:111
  1008.2 7.1 fusion.6
  1023.1 11.9 collective-permute-done
  1037.3 24.4 %conditional.5 = (bf16[128,1536]{1,0:T(8,128)(2,1)}, bf16[1,128,1536]{2,1,0:T(8,128)(2,1)}) conditional(s32[]{:T(128)} %convert_element_type.92, () %tuple.69, (bf16[128,1536]{1,0:T(8,128)(2,1)S(1)}, f32[4608]{0:T(1024)}, bf16[4,128,3072]{2,1,0:T(8,128)(2,1)}, bf16[4,128,3072]{2,1,0:T(8,128)(2,1)}, f32[1,128]{1,0:T(1,128)S(1)}, ...), branch_computations={%region_7.7_spmd, %region_8.10_spmd} | conditional | flops 1443506688 | bytes 69053088 | solution.py:158
  1040.5 4.7 copy.31
  1045.2 5.6 pad_maximum_fusion
  1052.3 3.3 bitcast_reduce_fusion
  1064.9 12.3 collective-permute-done.1
  1084.1 13.7 %conditional.4 = (bf16[128,12,128]{0,2,1:T(8,128)(2,1)}, bf16[128,3072]{1,0:T(8,128)(2,1)}, bf16[1,128,3072]{2,1,0:T(8,128)(2,1)}) conditional(s32[]{:T(128)} %convert_element_type.92, () %tuple.70, (bf16[128,1536]{1,0:T(8,128)(2,1)S(1)}, f32[4608]{0:T(1024)}, bf16[1536,4608]{1,0:T(8,128)(2,1)}, f32[1,128]{1,0:T(1,128)S(1)}) %tuple.71), branch_computations={%region_2.2_spmd, %region_3.6_spmd} | conditional | flops 1815284864 | bytes 26018840 | solution.py:111
  1085.3 7.1 fusion.6
  1100.2 11.9 collective-permute-done
  1114.4 24.4 %conditional.5 = (bf16[128,1536]{1,0:T(8,128)(2,1)}, bf16[1,128,1536]{2,1,0:T(8,128)(2,1)}) conditional(s32[]{:T(128)} %convert_element_type.92, () %tuple.69, (bf16[128,1536]{1,0:T(8,128)(2,1)S(1)}, f32[4608]{0:T(1024)}, bf16[4,128,3072]{2,1,0:T(8,128)(2,1)}, bf16[4,128,3072]{2,1,0:T(8,128)(2,1)}, f32[1,128]{1,0:T(1,128)S(1)}, ...), branch_computations={%region_7.7_spmd, %region_8.10_spmd} | conditional | flops 1443506688 | bytes 69053088 | solution.py:158
  1117.6 4.7 copy.31
  1122.3 5.6 pad_maximum_fusion
  1142.0 14.9 %collective-permute-done.1 = bf16[128,1536]{1,0:T(8,128)(2,1)S(1)} collective-permute-done((bf16[128,1536]{1,0:T(8,128)(2,1)}, bf16[128,1536]{1,0:T(8,128)(2,1)S(1)}, u32[]{:S(2)}, u32[]{:S(2)}) %collective-permute-start.1) | collective-permute-done | bytes 393248 | tf_op jit(solution)/shard_map/while/body/eval_jaxpr/ppermute | solution.py:34
  1163.8 13.7 %conditional.4 = (bf16[128,12,128]{0,2,1:T(8,128)(2,1)}, bf16[128,3072]{1,0:T(8,128)(2,1)}, bf16[1,128,3072]{2,1,0:T(8,128)(2,1)}) conditional(s32[]{:T(128)} %convert_element_type.92, () %tuple.70, (bf16[128,1536]{1,0:T(8,128)(2,1)S(1)}, f32[4608]{0:T(1024)}, bf16[1536,4608]{1,0:T(8,128)(2,1)}, f32[1,128]{1,0:T(1,128)S(1)}) %tuple.71), branch_computations={%region_2.2_spmd, %region_3.6_spmd} | conditional | flops 1815284864 | bytes 26018840 | solution.py:111
  1165.0 7.1 fusion.6
  1179.9 15.9 %collective-permute-done = bf16[128,3072]{1,0:T(8,128)(2,1)S(1)} collective-permute-done((bf16[128,3072]{1,0:T(8,128)(2,1)}, bf16[128,3072]{1,0:T(8,128)(2,1)S(1)}, u32[]{:S(2)}, u32[]{:S(2)}) %collective-permute-start) | collective-permute-done | bytes 786464 | tf_op jit(solution)/shard_map/while/body/eval_jaxpr/ppermute | solution.py:28
  1198.1 24.4 %conditional.5 = (bf16[128,1536]{1,0:T(8,128)(2,1)}, bf16[1,128,1536]{2,1,0:T(8,128)(2,1)}) conditional(s32[]{:T(128)} %convert_element_type.92, () %tuple.69, (bf16[128,1536]{1,0:T(8,128)(2,1)S(1)}, f32[4608]{0:T(1024)}, bf16[4,128,3072]{2,1,0:T(8,128)(2,1)}, bf16[4,128,3072]{2,1,0:T(8,128)(2,1)}, f32[1,128]{1,0:T(1,128)S(1)}, ...), branch_computations={%region_7.7_spmd, %region_8.10_spmd} | conditional | flops 1443506688 | bytes 69053088 | solution.py:158
  1201.2 4.7 copy.31
  1205.9 5.6 pad_maximum_fusion
  (276 shorter events, 281.7 us)
Async XLA Ops:
  7.2 3.8 copy-start
  17.7 13.5 %copy-start.1 = (f32[1,16,3,1536]{3,1,2,0:T(8,128)S(1)}, f32[1,16,3,1536]{3,1,2,0:T(8,128)}, u32[]{:S(2)}) copy-start(f32[1,16,3,1536]{3,1,2,0:T(8,128)} %param.22) | copy-start | bytes 884740
  17.7 420.7 %all-to-all-start = ((bf16[32,48,4608]{2,1,0:T(8,128)(2,1)}), bf16[32,48,4608]{2,1,0:T(8,128)(2,1)}, u32[]{:S(2)}, u32[]{:S(2)}) async-start(bf16[32,48,4608]{2,1,0:T(8,128)(2,1)} %stack.3), calls=%async_computation | async-start | bytes 28311552 | tf_op jit(solution)/shard_map/all_to_all | solution.py:21
  29.2 410.6 %copy-start.2 = (f32[1,128]{1,0:T(1,128)S(1)}, f32[1,128]{1,0:T(1,128)}, u32[]{:S(2)}) copy-start(f32[1,128]{1,0:T(1,128)} %param.20) | copy-start | bytes 1540
  29.2 410.6 %copy-start.3 = (s32[4]{0:T(128)S(1)}, s32[4]{0:T(128)}, u32[]{:S(2)}) copy-start(s32[4]{0:T(128)} %param.25) | copy-start | bytes 52
  29.2 410.5 %copy-start.4 = (s32[4]{0:T(128)S(1)}, s32[4]{0:T(128)}, u32[]{:S(2)}) copy-start(s32[4]{0:T(128)} %param.24) | copy-start | bytes 52
  29.2 410.5 %copy-start.5 = (f32[1,128]{1,0:T(1,128)S(1)}, f32[1,128]{1,0:T(1,128)}, u32[]{:S(2)}) copy-start(f32[1,128]{1,0:T(1,128)} %param.21) | copy-start | bytes 1540
  29.2 409.2 %all-gather.3.cloned.1.call-start = ((), (), s32[]{:S(2)}) async-start(), calls=%async_computation.1 | async-start | bytes 4866048 | tf_op jit(solution)/shard_map/all_gather | solution.py:59
  29.9 408.5 %collective-permute-start.2 = (bf16[4,128,3072]{2,1,0:T(8,128)(2,1)}, bf16[4,128,3072]{2,1,0:T(8,128)(2,1)}, u32[]{:S(2)}, u32[]{:S(2)}) collective-permute-start(bf16[4,128,3072]{2,1,0:T(8,128)(2,1)} %bitcast.20), channel_id=1, source_target_pairs={{0,1},{1,2},{2,3},{3,4},{4,5},{5,6},{6,7},{7,8},{8,9},{9,10},{10,1... | collective-permute-start | bytes 9437192 | tf_op jit(solution)/shard_map/ppermute | solution.py:28
  449.7 21.1 %collective-permute-start = (bf16[128,3072]{1,0:T(8,128)(2,1)}, bf16[128,3072]{1,0:T(8,128)(2,1)S(1)}, u32[]{:S(2)}, u32[]{:S(2)}) collective-permute-start(bf16[128,3072]{1,0:T(8,128)(2,1)} %get-tuple-element.585), channel_id=1, source_target_pairs={{0,1},{1,2},{2,3},{3,4},{4,5},{5,6},{6,7},{7,8},{8,9},{9,10},{10,1... | collective-permute-start | bytes 2359304 | tf_op jit(solution)/shard_map/while/body/eval_jaxpr/ppermute | solution.py:28
  474.6 5.7 collective-permute-start.1
  490.0 16.0 %collective-permute-start = (bf16[128,3072]{1,0:T(8,128)(2,1)}, bf16[128,3072]{1,0:T(8,128)(2,1)S(1)}, u32[]{:S(2)}, u32[]{:S(2)}) collective-permute-start(bf16[128,3072]{1,0:T(8,128)(2,1)} %get-tuple-element.585), channel_id=1, source_target_pairs={{0,1},{1,2},{2,3},{3,4},{4,5},{5,6},{6,7},{7,8},{8,9},{9,10},{10,1... | collective-permute-start | bytes 2359304 | tf_op jit(solution)/shard_map/while/body/eval_jaxpr/ppermute | solution.py:28
  509.8 17.6 %collective-permute-start.1 = (bf16[128,1536]{1,0:T(8,128)(2,1)}, bf16[128,1536]{1,0:T(8,128)(2,1)S(1)}, u32[]{:S(2)}, u32[]{:S(2)}) collective-permute-start(bf16[128,1536]{1,0:T(8,128)(2,1)} %get-tuple-element.587), channel_id=1, source_target_pairs={{0,32},{32,64},{64,96},{96,128},{128,160},{160,192},{192,224},{1,3... | collective-permute-start | bytes 1179656 | tf_op jit(solution)/shard_map/while/body/eval_jaxpr/ppermute | solution.py:34
  537.2 16.4 %collective-permute-start = (bf16[128,3072]{1,0:T(8,128)(2,1)}, bf16[128,3072]{1,0:T(8,128)(2,1)S(1)}, u32[]{:S(2)}, u32[]{:S(2)}) collective-permute-start(bf16[128,3072]{1,0:T(8,128)(2,1)} %get-tuple-element.585), channel_id=1, source_target_pairs={{0,1},{1,2},{2,3},{3,4},{4,5},{5,6},{6,7},{7,8},{8,9},{9,10},{10,1... | collective-permute-start | bytes 2359304 | tf_op jit(solution)/shard_map/while/body/eval_jaxpr/ppermute | solution.py:28
  557.3 10.4 collective-permute-start.1
  577.5 16.6 %collective-permute-start = (bf16[128,3072]{1,0:T(8,128)(2,1)}, bf16[128,3072]{1,0:T(8,128)(2,1)S(1)}, u32[]{:S(2)}, u32[]{:S(2)}) collective-permute-start(bf16[128,3072]{1,0:T(8,128)(2,1)} %get-tuple-element.585), channel_id=1, source_target_pairs={{0,1},{1,2},{2,3},{3,4},{4,5},{5,6},{6,7},{7,8},{8,9},{9,10},{10,1... | collective-permute-start | bytes 2359304 | tf_op jit(solution)/shard_map/while/body/eval_jaxpr/ppermute | solution.py:28
  597.9 10.2 collective-permute-start.1
  617.8 16.6 %collective-permute-start = (bf16[128,3072]{1,0:T(8,128)(2,1)}, bf16[128,3072]{1,0:T(8,128)(2,1)S(1)}, u32[]{:S(2)}, u32[]{:S(2)}) collective-permute-start(bf16[128,3072]{1,0:T(8,128)(2,1)} %get-tuple-element.585), channel_id=1, source_target_pairs={{0,1},{1,2},{2,3},{3,4},{4,5},{5,6},{6,7},{7,8},{8,9},{9,10},{10,1... | collective-permute-start | bytes 2359304 | tf_op jit(solution)/shard_map/while/body/eval_jaxpr/ppermute | solution.py:28
  638.2 10.2 collective-permute-start.1
  658.1 16.6 %collective-permute-start = (bf16[128,3072]{1,0:T(8,128)(2,1)}, bf16[128,3072]{1,0:T(8,128)(2,1)S(1)}, u32[]{:S(2)}, u32[]{:S(2)}) collective-permute-start(bf16[128,3072]{1,0:T(8,128)(2,1)} %get-tuple-element.585), channel_id=1, source_target_pairs={{0,1},{1,2},{2,3},{3,4},{4,5},{5,6},{6,7},{7,8},{8,9},{9,10},{10,1... | collective-permute-start | bytes 2359304 | tf_op jit(solution)/shard_map/while/body/eval_jaxpr/ppermute | solution.py:28
  678.5 10.2 collective-permute-start.1
  698.5 14.4 %collective-permute-start = (bf16[128,3072]{1,0:T(8,128)(2,1)}, bf16[128,3072]{1,0:T(8,128)(2,1)S(1)}, u32[]{:S(2)}, u32[]{:S(2)}) collective-permute-start(bf16[128,3072]{1,0:T(8,128)(2,1)} %get-tuple-element.585), channel_id=1, source_target_pairs={{0,1},{1,2},{2,3},{3,4},{4,5},{5,6},{6,7},{7,8},{8,9},{9,10},{10,1... | collective-permute-start | bytes 2359304 | tf_op jit(solution)/shard_map/while/body/eval_jaxpr/ppermute | solution.py:28
  716.6 208.3 %collective-permute-start.1 = (bf16[128,1536]{1,0:T(8,128)(2,1)}, bf16[128,1536]{1,0:T(8,128)(2,1)S(1)}, u32[]{:S(2)}, u32[]{:S(2)}) collective-permute-start(bf16[128,1536]{1,0:T(8,128)(2,1)} %get-tuple-element.587), channel_id=1, source_target_pairs={{0,32},{32,64},{64,96},{96,128},{128,160},{160,192},{192,224},{1,3... | collective-permute-start | bytes 1179656 | tf_op jit(solution)/shard_map/while/body/eval_jaxpr/ppermute | solution.py:34
  945.5 14.4 %collective-permute-start = (bf16[128,3072]{1,0:T(8,128)(2,1)}, bf16[128,3072]{1,0:T(8,128)(2,1)S(1)}, u32[]{:S(2)}, u32[]{:S(2)}) collective-permute-start(bf16[128,3072]{1,0:T(8,128)(2,1)} %get-tuple-element.585), channel_id=1, source_target_pairs={{0,1},{1,2},{2,3},{3,4},{4,5},{5,6},{6,7},{7,8},{8,9},{9,10},{10,1... | collective-permute-start | bytes 2359304 | tf_op jit(solution)/shard_map/while/body/eval_jaxpr/ppermute | solution.py:28
  977.2 6.0 slice-start
  980.5 2.7 slice-start.1
  986.5 13.5 %collective-permute-start.1 = (bf16[128,1536]{1,0:T(8,128)(2,1)}, bf16[128,1536]{1,0:T(8,128)(2,1)S(1)}, u32[]{:S(2)}, u32[]{:S(2)}) collective-permute-start(bf16[128,1536]{1,0:T(8,128)(2,1)} %get-tuple-element.587), channel_id=1, source_target_pairs={{0,32},{32,64},{64,96},{96,128},{128,160},{160,192},{192,224},{1,3... | collective-permute-start | bytes 1179656 | tf_op jit(solution)/shard_map/while/body/eval_jaxpr/ppermute | solution.py:34
  1020.7 14.4 %collective-permute-start = (bf16[128,3072]{1,0:T(8,128)(2,1)}, bf16[128,3072]{1,0:T(8,128)(2,1)S(1)}, u32[]{:S(2)}, u32[]{:S(2)}) collective-permute-start(bf16[128,3072]{1,0:T(8,128)(2,1)} %get-tuple-element.585), channel_id=1, source_target_pairs={{0,1},{1,2},{2,3},{3,4},{4,5},{5,6},{6,7},{7,8},{8,9},{9,10},{10,1... | collective-permute-start | bytes 2359304 | tf_op jit(solution)/shard_map/while/body/eval_jaxpr/ppermute | solution.py:28
  1052.3 6.0 slice-start
  1055.6 2.7 slice-start.1
  1061.7 15.5 %collective-permute-start.1 = (bf16[128,1536]{1,0:T(8,128)(2,1)}, bf16[128,1536]{1,0:T(8,128)(2,1)S(1)}, u32[]{:S(2)}, u32[]{:S(2)}) collective-permute-start(bf16[128,1536]{1,0:T(8,128)(2,1)} %get-tuple-element.587), channel_id=1, source_target_pairs={{0,32},{32,64},{64,96},{96,128},{128,160},{160,192},{192,224},{1,3... | collective-permute-start | bytes 1179656 | tf_op jit(solution)/shard_map/while/body/eval_jaxpr/ppermute | solution.py:34
  1097.8 14.4 %collective-permute-start = (bf16[128,3072]{1,0:T(8,128)(2,1)}, bf16[128,3072]{1,0:T(8,128)(2,1)S(1)}, u32[]{:S(2)}, u32[]{:S(2)}) collective-permute-start(bf16[128,3072]{1,0:T(8,128)(2,1)} %get-tuple-element.585), channel_id=1, source_target_pairs={{0,1},{1,2},{2,3},{3,4},{4,5},{5,6},{6,7},{7,8},{8,9},{9,10},{10,1... | collective-permute-start | bytes 2359304 | tf_op jit(solution)/shard_map/while/body/eval_jaxpr/ppermute | solution.py:28
  1129.4 6.0 slice-start
  1132.7 2.7 slice-start.1
  1138.8 18.1 %collective-permute-start.1 = (bf16[128,1536]{1,0:T(8,128)(2,1)}, bf16[128,1536]{1,0:T(8,128)(2,1)S(1)}, u32[]{:S(2)}, u32[]{:S(2)}) collective-permute-start(bf16[128,1536]{1,0:T(8,128)(2,1)} %get-tuple-element.587), channel_id=1, source_target_pairs={{0,32},{32,64},{64,96},{96,128},{128,160},{160,192},{192,224},{1,3... | collective-permute-start | bytes 1179656 | tf_op jit(solution)/shard_map/while/body/eval_jaxpr/ppermute | solution.py:34
  1177.5 18.3 %collective-permute-start = (bf16[128,3072]{1,0:T(8,128)(2,1)}, bf16[128,3072]{1,0:T(8,128)(2,1)S(1)}, u32[]{:S(2)}, u32[]{:S(2)}) collective-permute-start(bf16[128,3072]{1,0:T(8,128)(2,1)} %get-tuple-element.585), channel_id=1, source_target_pairs={{0,1},{1,2},{2,3},{3,4},{4,5},{5,6},{6,7},{7,8},{8,9},{9,10},{10,1... | collective-permute-start | bytes 2359304 | tf_op jit(solution)/shard_map/while/body/eval_jaxpr/ppermute | solution.py:28
  1213.1 6.0 slice-start
  1216.4 2.7 slice-start.1
  1222.5 3.8 collective-permute-start.1
Sparse Core Ops, SparseCore 0:
  32.6 156.9 all-gather.2
